TPU v7x, 32 devices: a whole 2x2x4 slice. The times are simulated.
32 devices in a mesh: sens: 4 (over y, x), slab: 8 (over z, core).
Axes of the slice: x: 2, y: 2, z: 4, core: 2. Of those that a mesh axis runs over, the one named last changes fastest.
Arguments:
- pressure: bfloat16 [32768, 128], P('slab'), may hold values from 0 to 1
- kernels: bfloat16 [4, 64, 256], replicated, may hold values from -0.0625 to 0.0625
- filter_gains: float32 [512], replicated, may hold values from 0.25 to 2
- measured: float32 [1024, 2, 512], P('sens'), may hold values from -6 to 6
- blocks: int32 [1024, 8, 64], P('sens', 'slab'), may hold values from 0 to 4095
- frames: int32 [1024, 8, 64], P('sens', 'slab'), may hold values from 0 to 2
- classes: int32 [1024, 8, 64], P('sens', 'slab'), may hold values from 0 to 3
- counts: int32 [1024, 8], P('sens', 'slab'), may hold values from 1 to 64, as said below
Outputs:
- residual: float32 [1024, 2, 512], P(('sens', 'slab'))
- gradient: float32 [32768, 128], P('slab', 'sens')
Inputs may be any that keep to these rules, and one draw needn't show every extreme that they name: counts[s, j] slots of sensor s in slab j are live; some sensor has all 64 slots live in some slab. `blocks`: slots at or past counts[s, j] are ignored.
All inputs are finite; a program needn't handle non-finite values.
Results may differ from a plain program's by a relative error of at most 0.00077.
Values may be sent and summed in bfloat16 or wider, within the bound.
No kernel may reach another device: no remote copies, remote signals or barrier semaphores. Data moves between devices by JAX's collectives and lax.ppermute only.
A program may use at most 256 MiB of HBM per device.

v0:
```python
import math
import jax
import jax.numpy as jnp
from jax import lax
from jax.sharding import PartitionSpec as P


def dft_pair(time_len):
    sample_ids = jnp.arange(time_len, dtype=jnp.int32)
    phase_ids = sample_ids[:, None] * sample_ids[None, :] % time_len
    angles = phase_ids.astype(jnp.float32) * (2.0 * math.pi / time_len)
    return (jnp.cos(angles), jnp.sin(angles))


def time_filter(traces, filter_gains, forward_basis, inverse_basis):
    time_len = filter_gains.shape[0]
    rows_flat = traces.reshape(-1, time_len)
    spectrum = jnp.dot(
        rows_flat,
        forward_basis,
        precision=lax.Precision.HIGHEST,
        preferred_element_type=jnp.float32,
    )
    spectrum = spectrum * jnp.concatenate([filter_gains, filter_gains])
    result = jnp.dot(
        spectrum, inverse_basis, precision=lax.Precision.HIGHEST, preferred_element_type=jnp.float32
    )
    return (result / time_len).reshape(traces.shape)


def per_device(pressure, kernels, filter_gains, measured, blocks, frames, classes, counts):
    kind_count, voxel_count, tap_count = kernels.shape
    block_count = pressure.shape[0]
    wave_count = pressure.shape[1] // voxel_count
    frame_len = tap_count // 2
    time_len = filter_gains.shape[0]
    frame_count = time_len // frame_len
    place_count = frame_count - 1
    combo_count = kind_count * place_count
    sensor_count, slot_count = (blocks.shape[0], blocks.shape[2])
    share_rows = sensor_count // lax.axis_size("slab")
    cosine_table, sine_table = dft_pair(time_len)
    forward_basis = jnp.concatenate([cosine_table, sine_table], axis=1)
    inverse_basis = jnp.concatenate([cosine_table, sine_table], axis=0)
    placed_list = []
    for offset in range(place_count):
        placed_list.append(
            jnp.pad(
                kernels,
                ((0, 0), (0, 0), (offset * frame_len, time_len - tap_count - offset * frame_len)),
            )
        )
    placed_kern = jnp.stack(placed_list, axis=1).reshape(combo_count, voxel_count, time_len)
    placed_wide = placed_kern.astype(jnp.float32)
    block_ids = blocks[:, 0, :]
    combo_ids = classes[:, 0, :] * place_count + frames[:, 0, :]
    live_slot = jnp.arange(slot_count, dtype=jnp.int32)[None, :] < counts[:, 0][:, None]
    combo_hot = (
        (combo_ids[:, :, None] == jnp.arange(combo_count, dtype=jnp.int32)) & live_slot[:, :, None]
    ).astype(jnp.bfloat16)
    block_range = jnp.arange(block_count, dtype=jnp.int32)
    picked_ids = block_ids.reshape(-1)
    row_hot = combo_hot
    picked = pressure[picked_ids].reshape(
        share_rows * lax.axis_size("slab"), slot_count, wave_count * voxel_count
    )
    grouped = jnp.einsum("skc,skx->scx", row_hot, picked, preferred_element_type=jnp.float32)
    grouped = grouped.reshape(
        share_rows * lax.axis_size("slab"), combo_count, wave_count, voxel_count
    )
    traces = lax.psum_scatter(
        jnp.einsum(
            "scwv,cvt->swt",
            grouped,
            placed_wide,
            precision=lax.Precision.HIGHEST,
            preferred_element_type=jnp.float32,
        ),
        "slab",
        scatter_dimension=0,
        tiled=True,
    )
    measured_share = lax.dynamic_slice_in_dim(
        measured, lax.axis_index("slab") * share_rows, share_rows, 0
    )
    residual = time_filter(traces, filter_gains, forward_basis, inverse_basis) - measured_share
    back_share = time_filter(residual, filter_gains, forward_basis, inverse_basis).astype(
        jnp.bfloat16
    )
    piece_rows = lax.all_gather(back_share, "slab", axis=0, tiled=True)
    row_count = piece_rows.shape[0]
    row_hot = combo_hot
    responses = jnp.einsum(
        "swt,cvt->scwv", piece_rows, placed_kern, preferred_element_type=jnp.float32
    )
    responses = responses.reshape(row_count * combo_count, wave_count * voxel_count)
    block_hot = (block_ids[:, :, None] == block_range).astype(jnp.bfloat16)
    tallies = jnp.einsum("skb,skc->bsc", block_hot, row_hot, preferred_element_type=jnp.float32)
    tallies = tallies.reshape(block_count, row_count * combo_count)
    partial_grad = jnp.dot(
        tallies, responses, precision=lax.Precision.HIGHEST, preferred_element_type=jnp.float32
    )
    gradient = lax.psum_scatter(partial_grad, "sens", scatter_dimension=1, tiled=True)
    return (residual, gradient)


def solution(mesh):
    return jax.shard_map(
        per_device,
        mesh=mesh,
        in_specs=(
            P("slab", None),
            P(),
            P(),
            P("sens", None, None),
            P("sens", "slab", None),
            P("sens", "slab", None),
            P("sens", "slab", None),
            P("sens", "slab"),
        ),
        out_specs=(P(("sens", "slab"), None, None), P("slab", "sens")),
        check_vma=False,
    )
```

profile of v0, /device:TPU:0, one launch (start us, length us, event | category | flops | bytes accessed | tf_op | source)
XLA Modules:
  0.0 294.1 jit_solution(7339451144219462057)
XLA Ops:
  7.2 0.0 copy-start
  7.2 0.0 reduce-scatter.3.cloned.1.call-start
  7.2 0.9 iota_compare_fusion.5
  8.1 0.9 add_bitcast_fusion
  9.0 0.1 copy.15
  9.1 0.9 copy.16
  10.0 0.1 reshape_squeeze.3
  10.2 0.1 compare_select_fusion
  10.2 1.1 pad_bitcast_fusion.2
  11.4 0.1 pad_maximum_fusion.16
  11.5 0.9 copy.18
  12.4 0.0 copy-done
  12.4 57.4 %gather_fusion = bf16[16384,128]{1,0:T(8,128)(2,1)} fusion(bf16[4096,128]{1,0:T(8,128)(2,1)S(1)} %copy-done, s32[16384]{0:T(1024)S(1)} %broadcast_clamp_fusion), kind=kCustom, calls=%fused_computation | custom fusion | bytes 8454144 | tf_op jit(solution)/shard_map/gather | solution.py:64
  69.8 3.4 %fusion.5 = f32[256,12,128]{2,1,0:T(8,128)S(1)} fusion(bf16[256,64,128]{2,1,0:T(8,128)(2,1)} %bitcast.41, s32[256,64]{1,0:T(8,128)S(1)} %copy.15, pred[256,64]{1,0:T(8,128)(4,1)S(1)} %iota_compare_fusion.5), kind=kOutput, calls=%fused_computation.9 | convolution fusion | flops 50724864 | bytes 5849088 | tf_op jit(solution)/shard_map/skc,skx->scx/dot_general | solution.py:67
  73.2 0.0 copy-start.2
  73.2 1.6 copy.17
  74.8 0.0 copy-done.2
  74.8 0.0 copy-start.5
  74.8 3.8 %convolution_bitcast_fusion.1 = f32[256,2,512]{2,0,1:T(8,128)} fusion(f32[256,12,2,64]{0,3,2,1:T(8,128)} %bitcast.44, bf16[12,64,512,1]{2,1,3,0:T(8,128)(2,1)S(1)} %bitcast.42), kind=kOutput, calls=%fused_computation.18 | convolution fusion | flops 2415919104 | bytes 3407872 | tf_op jit(solution)/shard_map/scwv,cvt->swt/dot_general | solution.py:72
  78.7 0.0 reduce-scatter.3.cloned.1.call-update
  78.7 0.0 reduce-scatter.5.cloned.1.call-start
  78.8 0.0 copy-done.5
  78.8 0.1 copy.21
  78.9 46.5 %fusion.2 = f32[4096,256,12]{0,2,1:T(8,128)} fusion(s32[256,64]{1,0:T(8,128)S(1)} %copy.21, s32[256,64]{1,0:T(8,128)S(1)} %copy.15, pred[256,64]{1,0:T(8,128)(4,1)S(1)} %iota_compare_fusion.5), kind=kOutput, calls=%fused_computation.4 | convolution fusion | flops 1678114816 | bytes 50479104 | tf_op jit(solution)/shard_map/skb,skc->bsc/dot_general | solution.py:98
  125.4 0.0 copy-start.6
  125.4 54.3 %reshape.100 = f32[4096,3072]{0,1:T(8,128)} reshape(f32[4096,256,12]{0,2,1:T(8,128)} %fusion.2) | data formatting | bytes 100663296 | tf_op jit(solution)/shard_map/reshape | solution.py:99
  179.6 0.0 copy-done.6
  179.6 4.1 %fusion.27 = (f32[512,512]{1,0:T(8,128)S(1)}, f32[512,512]{1,0:T(8,128)S(1)}) fusion(), kind=kLoop, calls=%fused_computation.36 | loop fusion | flops 3670016 | bytes 2097152 | tf_op jit(solution)/shard_map/sin | solution.py:12
  183.7 0.0 reduce-scatter.3.cloned.1.call-done
  183.8 1.0 copy.20
  184.8 0.1 reshape.98
  184.9 1.4 fusion.11
  186.2 1.4 fusion.13
  187.6 0.1 reshape.99
  187.7 1.0 dynamic-slice_subtract_fusion
  188.7 0.0 copy-start.4
  188.7 0.1 reshape.101
  188.8 1.4 fusion.12
  190.2 0.0 copy-start.3
  190.2 1.4 fusion.15
  191.6 0.0 copy-done.4
  191.6 16.6 %all_gather.3 = bf16[256,2,512]{2,0,1:T(8,128)(2,1)S(1)} all-gather(bf16[32,2,512]{2,0,1:T(8,128)(2,1)S(1)} %copy.22), channel_id=1, replica_groups=mesh['sens'=4,'slab'=8] {'slab'}, dimensions={0}, use_global_device_ids=true | all-gather | bytes 589824 | tf_op jit(solution)/shard_map/all_gather | solution.py:90
  208.2 0.0 copy-done.3
  208.2 0.6 convolution_bitcast_fusion
  208.8 3.7 %copy.23 = f32[256,12,2,64]{3,2,1,0:T(2,128)} copy(f32[256,12,2,64]{0,3,2,1:T(8,128)S(1)} %convolution_bitcast_fusion) | data formatting | bytes 3145728 | tf_op jit(solution)/shard_map/swt,cvt->scwv/transpose | solution.py:93
  212.6 3.4 %reshape.102 = f32[3072,128]{1,0:T(8,128)S(1)} reshape(f32[256,12,2,64]{3,2,1,0:T(2,128)} %copy.23) | data formatting | bytes 3145728 | tf_op jit(solution)/shard_map/reshape | solution.py:96
  215.9 0.0 copy-start.1
  216.0 34.9 %fusion.33 = f32[4096,128]{0,1:T(8,128)} fusion(f32[4096,3072]{0,1:T(8,128)} %reshape.100, f32[3072,128]{1,0:T(8,128)S(1)} %reshape.102), kind=kOutput, calls=%fused_computation.51 | convolution fusion | flops 19327352832 | bytes 54001664 | tf_op jit(solution)/shard_map/dot_general | solution.py:100
  250.9 0.0 reduce-scatter.5.cloned.1.call-update
  250.9 36.4 %reduce-scatter.5.cloned.1.call-done = f32[4096,32]{0,1:T(8,128)} async-done(((f32[4096,128]{0,1:T(8,128)}), f32[4096,32]{0,1:T(8,128)}) %reduce-scatter.5.cloned.1.call-update) | async-done | bytes 524304 | tf_op jit(solution)/shard_map/reduce_scatter | solution.py:103
  287.3 0.0 copy-done.1
  (4 shorter events, 0.1 us)
Async XLA Ops:
  7.2 5.2 %copy-start = (bf16[4096,128]{1,0:T(8,128)(2,1)S(1)}, bf16[4096,128]{1,0:T(8,128)(2,1)}, u32[]{:S(2)}) copy-start(bf16[4096,128]{1,0:T(8,128)(2,1)} %param.8) | copy-start | bytes 3145732
  7.2 176.6 %reduce-scatter.3.cloned.1.call-start = ((), (), s32[]{:S(2)}) async-start(), calls=%async_computation.2 | async-start | bytes 1179648 | tf_op jit(solution)/shard_map/reduce_scatter | solution.py:71
  73.2 1.6 copy-start.2
  74.8 3.9 %copy-start.5 = (s32[256,1,64]{0,2,1:T(8,128)S(1)}, s32[256,1,64]{0,2,1:T(8,128)}, u32[]{:S(2)}) copy-start(s32[256,1,64]{0,2,1:T(8,128)} %param.12) | copy-start | bytes 196612
  78.7 208.6 %reduce-scatter.5.cloned.1.call-start = ((), (), s32[]{:S(2)}) async-start(), calls=%async_computation.3 | async-start | bytes 2621440 | tf_op jit(solution)/shard_map/reduce_scatter | solution.py:103
  125.4 54.3 %copy-start.6 = (f32[512]{0:T(512)S(1)}, f32[512]{0:T(512)}, u32[]{:S(2)}) copy-start(f32[512]{0:T(512)} %param.10) | copy-start | bytes 6148
  188.7 2.9 copy-start.4
  190.2 18.0 %copy-start.3 = (bf16[4,3,64,512]{3,2,1,0:T(8,128)(2,1)S(1)}, bf16[4,3,64,512]{3,2,1,0:T(8,128)(2,1)}, u32[]{:S(2)}) copy-start(bf16[4,3,64,512]{3,2,1,0:T(8,128)(2,1)} %copy.18) | copy-start | bytes 2359300
  215.9 71.3 %copy-start.1 = (bf16[4096,128]{1,0:T(8,128)(2,1)S(1)}, bf16[4096,128]{1,0:T(8,128)(2,1)}, u32[]{:S(2)}) copy-start(bf16[4096,128]{1,0:T(8,128)(2,1)} %param.8) | copy-start | bytes 3145732
Sparse Core Ops, SparseCore 0:
  78.8 34.8 reduce-scatter.2
  251.0 36.1 reduce-scatter.4
where the time goes:
time: 295 us; the launch traced here: 294 us
  local copies, waits for them, and re-layouts  125 us (42%)
  matrix products  94.8 us (32%)
  waiting for transfers between devices  36.4 us (12%)
  blocking collectives  16.6 us (6%)
  between operations  14.2 us (5%)
  other arithmetic  6.99 us (2%)
    gather x1, local copies, waits for them, and re-layouts, per_device(): pressure[picked_ids]  57.4 us
    reshape x1, local copies, waits for them, and re-layouts, per_device(): tallies = tallies.reshape(block_count, row_count * combo_count)  54.3 us
    dot_general x1, matrix products, per_device(): jnp.einsum('skb,skc->bsc', block_hot, row_hot, preferred_element_type=jnp...  46.5 us
    reduce_scatter x1, waiting for transfers between devices, per_device(): lax.psum_scatter(partial_grad, 'sens', scatter_dimension=1, tiled=True)  36.4 us
    dot_general x1, matrix products, per_device(): jnp.dot(tallies, responses, precision=lax.Precision.HIGHEST, preferred_el...  34.9 us
    all_gather x1, blocking collectives, per_device(): piece_rows = lax.all_gather(back_share, 'slab', axis=0, tiled=True)  16.6 us
  transfers between devices with their start and end apart: 2, of which 1 were waited for; matrix products, arithmetic and copies ran while one was open for 36% of the time, Pallas kernels for 0%

commit v1 on v0

--- a/solution.py
+++ b/solution.py
@@ -87,7 +87,14 @@
     back_share = time_filter(residual, filter_gains, forward_basis, inverse_basis).astype(
         jnp.bfloat16
     )
-    piece_rows = lax.all_gather(back_share, "slab", axis=0, tiled=True)
+    x = back_share
+    ways, here, lap = (lax.axis_size("slab"), lax.axis_index("slab"), x.shape[0])
+    shape = [n * ways if d == 0 else n for d, n in enumerate(x.shape)]
+    full = lax.dynamic_update_slice_in_dim(jnp.zeros(shape, x.dtype), x, here * lap, axis=0)
+    for far in range(1, ways):
+        x = lax.ppermute(x, "slab", [(d, (d + 1) % ways) for d in range(ways)])
+        full = lax.dynamic_update_slice_in_dim(full, x, (here - far) % ways * lap, axis=0)
+    piece_rows = full
     row_count = piece_rows.shape[0]
     row_hot = combo_hot
     responses = jnp.einsum(

time: 295 us -> 340 us (1.15)
  waiting for transfers between devices: 36.4 us -> 97.2 us
  blocking collectives: 16.6 us -> 0 us
    ppermute x0 -> x7, waiting for transfers between devices: none -> 32.8 us  [per_device(): x = lax.ppermute(x, 'slab', [(d, (d + 1) % ways) for d in range(ways)])]
    reduce_scatter x1, waiting for transfers between devices: 0.02 us -> 30.7 us  [per_device(): lax.psum_scatter(jnp.einsum('scwv,cvt->swt', grouped, placed_wide, precis...]
    all_gather x1 -> x0, blocking collectives: 16.6 us -> none  [per_device(): piece_rows = lax.all_gather(back_share, 'slab', axis=0, tiled=True)]
  transfers between devices with their start and end apart: 2 -> 9, of which waited for: 1 -> 8; matrix products, arithmetic and copies ran while one was open for 36% -> 31% of each run, Pallas kernels for 0% -> 0%
where the time goes in v1:
time: 340 us; the launch traced here: 339 us
  local copies, waits for them, and re-layouts  125 us (37%)
  waiting for transfers between devices  97.2 us (29%)
  matrix products  94.8 us (28%)
  between operations  14.3 us (4%)
  other arithmetic  7 us (2%)
    gather x1, local copies, waits for them, and re-layouts, per_device(): pressure[picked_ids]  57.4 us
    reshape x1, local copies, waits for them, and re-layouts, per_device(): tallies = tallies.reshape(block_count, row_count * combo_count)  54.3 us
    dot_general x1, matrix products, per_device(): jnp.einsum('skb,skc->bsc', block_hot, row_hot, preferred_element_type=jnp...  46.5 us
    dot_general x1, matrix products, per_device(): jnp.dot(tallies, responses, precision=lax.Precision.HIGHEST, preferred_el...  35 us
    reduce_scatter x1, waiting for transfers between devices, per_device(): lax.psum_scatter(partial_grad, 'sens', scatter_dimension=1, tiled=True)  33.6 us
    ppermute x7, waiting for transfers between devices, per_device(): x = lax.ppermute(x, 'slab', [(d, (d + 1) % ways) for d in range(ways)])  32.8 us
    reduce_scatter x1, waiting for transfers between devices, per_device(): lax.psum_scatter(jnp.einsum('scwv,cvt->swt', grouped, placed_wide, precis...  30.7 us
  transfers between devices with their start and end apart: 9, of which 8 were waited for; matrix products, arithmetic and copies ran while one was open for 31% of the time, Pallas kernels for 0%

profile of v1, /device:TPU:0, one launch (start us, length us, event | category | flops | bytes accessed | tf_op | source)
XLA Modules:
  0.0 338.8 jit_solution(4953304172154507191)
XLA Ops:
  7.2 0.0 copy-start
  7.2 0.0 reduce-scatter.3.cloned.1.call-start
  7.2 0.9 iota_compare_fusion.5
  8.1 0.0 copy-start.5
  8.1 0.9 add_bitcast_fusion
  9.0 0.1 copy.16
  9.1 0.9 copy.17
  10.0 0.1 reshape_squeeze.3
  10.2 0.1 compare_select_fusion
  10.3 1.1 pad_bitcast_fusion.2
  11.4 0.1 pad_maximum_fusion.16
  11.5 0.9 copy.19
  12.4 0.0 copy-done
  12.4 57.4 %gather_fusion = bf16[16384,128]{1,0:T(8,128)(2,1)} fusion(bf16[4096,128]{1,0:T(8,128)(2,1)S(1)} %copy-done, s32[16384]{0:T(1024)S(1)} %broadcast_clamp_fusion), kind=kCustom, calls=%fused_computation | custom fusion | bytes 8454144 | tf_op jit(solution)/shard_map/gather | solution.py:64
  69.8 0.0 copy-done.5
  69.8 3.4 fusion.5
  73.2 1.6 copy.18
  74.8 0.0 copy-done.2
  74.8 0.0 copy-start.7
  74.8 3.9 %convolution_bitcast_fusion.1 = f32[256,2,512]{2,0,1:T(8,128)} fusion(f32[256,12,2,64]{0,3,2,1:T(8,128)} %bitcast.44, bf16[12,64,512,1]{2,1,3,0:T(8,128)(2,1)S(1)} %bitcast.42), kind=kOutput, calls=%fused_computation.18 | convolution fusion | flops 2415919104 | bytes 3407872 | tf_op jit(solution)/shard_map/scwv,cvt->swt/dot_general | solution.py:72
  78.7 0.0 reduce-scatter.3.cloned.1.call-update
  78.7 0.2 reduce-scatter.5.cloned.1.call-start
  79.0 0.0 copy-done.7
  79.0 0.1 copy.22
  79.1 0.0 copy-done.8
  79.1 4.1 %fusion.27 = (f32[512,512]{1,0:T(8,128)S(1)}, f32[512,512]{1,0:T(8,128)S(1)}) fusion(), kind=kLoop, calls=%fused_computation.36 | loop fusion | flops 3670016 | bytes 2097152 | tf_op jit(solution)/shard_map/sin | solution.py:12
  83.2 30.7 %reduce-scatter.3.cloned.1.call-done = f32[32,2,512]{2,0,1:T(8,128)} async-done(((f32[256,2,512]{2,0,1:T(8,128)}), f32[32,2,512]{2,0,1:T(8,128)}) %reduce-scatter.3.cloned.1.call-update) | async-done | bytes 131088 | tf_op jit(solution)/shard_map/reduce_scatter | solution.py:71
  113.9 1.0 copy.21
  114.9 0.1 reshape.98
  115.0 1.4 fusion.11
  116.4 1.4 fusion.13
  117.8 0.1 reshape.99
  117.9 1.0 dynamic-slice_subtract_fusion
  118.8 0.0 copy-start.4
  118.9 0.1 reshape.101
  119.0 1.4 fusion.12
  120.3 1.4 fusion.15
  121.7 0.0 copy-done.4
  121.8 0.3 collective-permute-start
  122.1 0.0 copy-done.6
  122.1 46.5 %fusion.2 = f32[4096,256,12]{0,2,1:T(8,128)} fusion(s32[256,64]{1,0:T(8,128)S(1)} %copy.22, s32[256,64]{1,0:T(8,128)S(1)} %copy.16, pred[256,64]{1,0:T(8,128)(4,1)S(1)} %copy-done.6), kind=kOutput, calls=%fused_computation.4 | convolution fusion | flops 1678114816 | bytes 50479104 | tf_op jit(solution)/shard_map/skb,skc->bsc/dot_general | solution.py:105
  168.6 54.3 %reshape.100 = f32[4096,3072]{0,1:T(8,128)} reshape(f32[4096,256,12]{0,2,1:T(8,128)} %fusion.2) | data formatting | bytes 100663296 | tf_op jit(solution)/shard_map/reshape | solution.py:106
  222.9 0.0 collective-permute-done
  222.9 0.0 collective-permute-start.1
  223.0 5.5 %collective-permute-done.1 = bf16[32,2,512]{2,0,1:T(8,128)(2,1)S(1)} collective-permute-done((bf16[32,2,512]{2,0,1:T(8,128)(2,1)S(1)}, bf16[32,2,512]{2,0,1:T(8,128)(2,1)S(1)}, u32[]{:S(2)}, u32[]{:S(2)}) %collective-permute-start.1) | collective-permute-done | bytes 65568 | tf_op jit(solution)/shard_map/ppermute | solution.py:95
  228.4 0.0 collective-permute-start.2
  228.5 5.5 %collective-permute-done.2 = bf16[32,2,512]{2,0,1:T(8,128)(2,1)S(1)} collective-permute-done((bf16[32,2,512]{2,0,1:T(8,128)(2,1)S(1)}, bf16[32,2,512]{2,0,1:T(8,128)(2,1)S(1)}, u32[]{:S(2)}, u32[]{:S(2)}) %collective-permute-start.2) | collective-permute-done | bytes 65568 | tf_op jit(solution)/shard_map/ppermute | solution.py:95
  233.9 0.0 collective-permute-start.3
  233.9 5.5 %collective-permute-done.3 = bf16[32,2,512]{2,0,1:T(8,128)(2,1)S(1)} collective-permute-done((bf16[32,2,512]{2,0,1:T(8,128)(2,1)S(1)}, bf16[32,2,512]{2,0,1:T(8,128)(2,1)S(1)}, u32[]{:S(2)}, u32[]{:S(2)}) %collective-permute-start.3) | collective-permute-done | bytes 65568 | tf_op jit(solution)/shard_map/ppermute | solution.py:95
  239.4 0.0 collective-permute-start.4
  239.4 5.5 %collective-permute-done.4 = bf16[32,2,512]{2,0,1:T(8,128)(2,1)S(1)} collective-permute-done((bf16[32,2,512]{2,0,1:T(8,128)(2,1)S(1)}, bf16[32,2,512]{2,0,1:T(8,128)(2,1)S(1)}, u32[]{:S(2)}, u32[]{:S(2)}) %collective-permute-start.4) | collective-permute-done | bytes 65568 | tf_op jit(solution)/shard_map/ppermute | solution.py:95
  244.9 0.0 collective-permute-start.5
  244.9 5.5 %collective-permute-done.5 = bf16[32,2,512]{2,0,1:T(8,128)(2,1)S(1)} collective-permute-done((bf16[32,2,512]{2,0,1:T(8,128)(2,1)S(1)}, bf16[32,2,512]{2,0,1:T(8,128)(2,1)S(1)}, u32[]{:S(2)}, u32[]{:S(2)}) %collective-permute-start.5) | collective-permute-done | bytes 65568 | tf_op jit(solution)/shard_map/ppermute | solution.py:95
  250.4 0.0 collective-permute-start.6
  250.4 5.5 %collective-permute-done.6 = bf16[32,2,512]{2,0,1:T(8,128)(2,1)S(1)} collective-permute-done((bf16[32,2,512]{2,0,1:T(8,128)(2,1)S(1)}, bf16[32,2,512]{2,0,1:T(8,128)(2,1)S(1)}, u32[]{:S(2)}, u32[]{:S(2)}) %collective-permute-start.6) | collective-permute-done | bytes 65568 | tf_op jit(solution)/shard_map/ppermute | solution.py:95
  255.9 0.0 copy-done.3
  255.9 0.6 convolution_bitcast_fusion
  256.5 3.5 %copy.25 = f32[256,12,2,64]{3,2,1,0:T(2,128)} copy(f32[256,12,2,64]{0,3,2,1:T(8,128)S(1)} %convolution_bitcast_fusion) | data formatting | bytes 3145728 | tf_op jit(solution)/shard_map/swt,cvt->scwv/transpose | solution.py:100
  260.0 3.4 reshape.102
  263.4 0.0 copy-start.1
  263.4 35.0 %fusion.34 = f32[4096,128]{0,1:T(8,128)} fusion(f32[4096,3072]{0,1:T(8,128)} %reshape.100, f32[3072,128]{1,0:T(8,128)S(1)} %reshape.102), kind=kOutput, calls=%fused_computation.60 | convolution fusion | flops 19327352832 | bytes 54001664 | tf_op jit(solution)/shard_map/dot_general | solution.py:107
  298.3 0.0 reduce-scatter.5.cloned.1.call-update
  298.4 33.6 %reduce-scatter.5.cloned.1.call-done = f32[4096,32]{0,1:T(8,128)} async-done(((f32[4096,128]{0,1:T(8,128)}), f32[4096,32]{0,1:T(8,128)}) %reduce-scatter.5.cloned.1.call-update) | async-done | bytes 524304 | tf_op jit(solution)/shard_map/reduce_scatter | solution.py:110
  332.0 0.0 copy-done.1
  (16 shorter events, 0.2 us)
Async XLA Ops:
  7.2 5.3 %copy-start = (bf16[4096,128]{1,0:T(8,128)(2,1)S(1)}, bf16[4096,128]{1,0:T(8,128)(2,1)}, u32[]{:S(2)}) copy-start(bf16[4096,128]{1,0:T(8,128)(2,1)} %param.8) | copy-start | bytes 3145732
  7.2 106.7 %reduce-scatter.3.cloned.1.call-start = ((), (), s32[]{:S(2)}) async-start(), calls=%async_computation.2 | async-start | bytes 1179648 | tf_op jit(solution)/shard_map/reduce_scatter | solution.py:71
  8.1 61.7 %copy-start.5 = (pred[256,64]{1,0:T(8,128)(4,1)}, pred[256,64]{1,0:T(8,128)(4,1)S(1)}, u32[]{:S(2)}) copy-start(pred[256,64]{1,0:T(8,128)(4,1)S(1)} %iota_compare_fusion.5) | copy-start | bytes 49156
  73.2 1.6 copy-start.2
  74.8 4.1 %copy-start.7 = (s32[256,1,64]{0,2,1:T(8,128)S(1)}, s32[256,1,64]{0,2,1:T(8,128)}, u32[]{:S(2)}) copy-start(s32[256,1,64]{0,2,1:T(8,128)} %param.12) | copy-start | bytes 196612
  74.8 4.2 %copy-start.8 = (f32[512]{0:T(512)S(1)}, f32[512]{0:T(512)}, u32[]{:S(2)}) copy-start(f32[512]{0:T(512)} %param.10) | copy-start | bytes 6148
  78.7 253.2 %reduce-scatter.5.cloned.1.call-start = ((), (), s32[]{:S(2)}) async-start(), calls=%async_computation.3 | async-start | bytes 2621440 | tf_op jit(solution)/shard_map/reduce_scatter | solution.py:110
  118.8 2.9 copy-start.4
  120.3 1.8 copy-start.6
  121.8 101.1 %collective-permute-start = (bf16[32,2,512]{2,0,1:T(8,128)(2,1)S(1)}, bf16[32,2,512]{2,0,1:T(8,128)(2,1)S(1)}, u32[]{:S(2)}, u32[]{:S(2)}) collective-permute-start(bf16[32,2,512]{2,0,1:T(8,128)(2,1)S(1)} %get-tuple-element.5), channel_id=1, source_target_pairs={{0,1},{1,2},{2,3},{3,4},{4,5},{5,6},{6,7},{7,0},{8,9},{9,10},{10,1... | collective-permute-start | bytes 196616 | tf_op jit(solution)/shard_map/ppermute | solution.py:95
  168.6 87.3 %copy-start.3 = (bf16[4,3,64,512]{3,2,1,0:T(8,128)(2,1)S(1)}, bf16[4,3,64,512]{3,2,1,0:T(8,128)(2,1)}, u32[]{:S(2)}) copy-start(bf16[4,3,64,512]{3,2,1,0:T(8,128)(2,1)} %copy.19) | copy-start | bytes 2359300
  222.9 5.5 %collective-permute-start.1 = (bf16[32,2,512]{2,0,1:T(8,128)(2,1)S(1)}, bf16[32,2,512]{2,0,1:T(8,128)(2,1)S(1)}, u32[]{:S(2)}, u32[]{:S(2)}) collective-permute-start(bf16[32,2,512]{2,0,1:T(8,128)(2,1)S(1)} %collective-permute-done), channel_id=1, source_target_pairs={{0,1},{1,2},{2,3},{3,4},{4,5},{5,6},{6,7},{7,0},{8,9},{9,10},{10,1... | collective-permute-start | bytes 196616 | tf_op jit(solution)/shard_map/ppermute | solution.py:95
  228.4 5.5 %collective-permute-start.2 = (bf16[32,2,512]{2,0,1:T(8,128)(2,1)S(1)}, bf16[32,2,512]{2,0,1:T(8,128)(2,1)S(1)}, u32[]{:S(2)}, u32[]{:S(2)}) collective-permute-start(bf16[32,2,512]{2,0,1:T(8,128)(2,1)S(1)} %collective-permute-done.1), channel_id=1, source_target_pairs={{0,1},{1,2},{2,3},{3,4},{4,5},{5,6},{6,7},{7,0},{8,9},{9,10},{10,1... | collective-permute-start | bytes 196616 | tf_op jit(solution)/shard_map/ppermute | solution.py:95
  233.9 5.5 %collective-permute-start.3 = (bf16[32,2,512]{2,0,1:T(8,128)(2,1)S(1)}, bf16[32,2,512]{2,0,1:T(8,128)(2,1)S(1)}, u32[]{:S(2)}, u32[]{:S(2)}) collective-permute-start(bf16[32,2,512]{2,0,1:T(8,128)(2,1)S(1)} %collective-permute-done.2), channel_id=1, source_target_pairs={{0,1},{1,2},{2,3},{3,4},{4,5},{5,6},{6,7},{7,0},{8,9},{9,10},{10,1... | collective-permute-start | bytes 196616 | tf_op jit(solution)/shard_map/ppermute | solution.py:95
  239.4 5.5 %collective-permute-start.4 = (bf16[32,2,512]{2,0,1:T(8,128)(2,1)S(1)}, bf16[32,2,512]{2,0,1:T(8,128)(2,1)S(1)}, u32[]{:S(2)}, u32[]{:S(2)}) collective-permute-start(bf16[32,2,512]{2,0,1:T(8,128)(2,1)S(1)} %collective-permute-done.3), channel_id=1, source_target_pairs={{0,1},{1,2},{2,3},{3,4},{4,5},{5,6},{6,7},{7,0},{8,9},{9,10},{10,1... | collective-permute-start | bytes 196616 | tf_op jit(solution)/shard_map/ppermute | solution.py:95
  244.9 5.5 %collective-permute-start.5 = (bf16[32,2,512]{2,0,1:T(8,128)(2,1)S(1)}, bf16[32,2,512]{2,0,1:T(8,128)(2,1)S(1)}, u32[]{:S(2)}, u32[]{:S(2)}) collective-permute-start(bf16[32,2,512]{2,0,1:T(8,128)(2,1)S(1)} %collective-permute-done.4), channel_id=1, source_target_pairs={{0,1},{1,2},{2,3},{3,4},{4,5},{5,6},{6,7},{7,0},{8,9},{9,10},{10,1... | collective-permute-start | bytes 196616 | tf_op jit(solution)/shard_map/ppermute | solution.py:95
  250.4 5.5 %collective-permute-start.6 = (bf16[32,2,512]{2,0,1:T(8,128)(2,1)S(1)}, bf16[32,2,512]{2,0,1:T(8,128)(2,1)S(1)}, u32[]{:S(2)}, u32[]{:S(2)}) collective-permute-start(bf16[32,2,512]{2,0,1:T(8,128)(2,1)S(1)} %collective-permute-done.5), channel_id=1, source_target_pairs={{0,1},{1,2},{2,3},{3,4},{4,5},{5,6},{6,7},{7,0},{8,9},{9,10},{10,1... | collective-permute-start | bytes 196616 | tf_op jit(solution)/shard_map/ppermute | solution.py:95
  263.4 68.6 %copy-start.1 = (bf16[4096,128]{1,0:T(8,128)(2,1)S(1)}, bf16[4096,128]{1,0:T(8,128)(2,1)}, u32[]{:S(2)}) copy-start(bf16[4096,128]{1,0:T(8,128)(2,1)} %param.8) | copy-start | bytes 3145732
Sparse Core Ops, SparseCore 0:
  78.8 35.0 reduce-scatter.2
  298.5 33.4 reduce-scatter.4
